TPU v7x, 32 devices: a whole 2x2x4 slice. The times are simulated.
32 devices in a mesh: group: 2 (over y), ctx: 4 (over z), head: 2 (over x), req: 2 (over core).
Axes of the slice: x: 2, y: 2, z: 4, core: 2. Of those that a mesh axis runs over, the one named last changes fastest.
Arguments:
- kda_query: bfloat16 [4, 768, 4096], P(('group', 'req'), 'ctx', 'head'), parts along dimension 0, may hold values from -6 to 6
- kda_key: bfloat16 [4, 768, 4096], P(('group', 'req'), 'ctx', 'head'), parts along dimension 0, may hold values from -6 to 6
- kda_value: bfloat16 [4, 768, 4096], P(('group', 'req'), 'ctx', 'head'), parts along dimension 0, may hold values from -6 to 6
- log_decay: bfloat16 [4, 768, 4096], P(('group', 'req'), 'ctx', 'head'), parts along dimension 0, may hold values from -1 to 0
- write_strength: float32 [4, 32, 768], P(('group', 'req'), 'head', 'ctx'), parts along dimension 0, may hold values from 0.1 to 0.95
- mla_query: bfloat16 [4, 768, 18432], P(('group', 'req'), 'ctx', 'head'), parts along dimension 0, may hold values from -18 to 18
- latents: bfloat16 [4, 768, 576], P(('group', 'req'), 'ctx'), parts along dimension 0, may hold values from -8 to 8
- value_up: bfloat16 [32, 512, 128], P('head'), may hold values from -0.25 to 0.25
- out_proj: bfloat16 [4096, 2304], P('head'), may hold values from -0.09375 to 0.09375
- doc_lengths: int32 [4, 8], P(('group', 'req')), parts along dimension 0, may hold values from 1 to 288, 768 in all within a row
Outputs:
- kda_out: bfloat16 [4, 768, 4096], P(('group', 'req'), 'ctx', 'head'), parts along dimension 0
- mixed: bfloat16 [4, 768, 2304], P(('group', 'req'), ('ctx', 'head')), parts along dimension 0
There are 2 independent parts, one for each index of `group`. A program takes and returns all parts, laid end to end along the dimension named above; an argument that names none is the same for every part. Nothing has to cross between parts.
Inputs may be any that keep to these rules, and one draw needn't show every extreme that they name: `doc_lengths`: each row's lengths sum to 768, and each row's longest prompt has exactly 288 positions.
All inputs are finite; a program needn't handle non-finite values.
Results may differ from a plain program's by a relative error of at most 0.009.
Values may be sent and summed in bfloat16 or wider, within the bound.
A program may use at most 128 MiB of HBM per device.

v0:
```python
import math
import jax
import jax.numpy as jnp
from jax import lax
from jax.sharding import PartitionSpec as P

ROPE = 64
NOPE = 128
SPAN = 64
top_value = lax.Precision.HIGHEST
masked_score = -1e30


def from_behind(value, axis, by):
    peers = lax.axis_size(axis)
    pairs = [(i, i + by) for i in range(peers) if 0 <= i + by < peers]
    return lax.ppermute(value, axis, pairs)


def unit_length(values):
    return values * lax.rsqrt(jnp.sum(values * values, axis=-1, keepdims=True) + 1e-06)


def doc_index(position_list, doc_ends):
    return jnp.sum((doc_ends[None, :] <= position_list[:, None]).astype(jnp.int32), axis=1)


def span_terms(query_rows, key_rows, value_rows, decay_rows, strength, doc_ids, prev_doc):
    span_len = key_rows.shape[1]
    state_dim = key_rows.shape[2]
    row_index = jnp.arange(span_len, dtype=jnp.int32)
    inclusive = (row_index[:, None] >= row_index[None, :]).astype(jnp.float32)
    summed = jnp.einsum("ij,hjc->hic", inclusive, decay_rows, precision=top_value)
    growth = jnp.exp(summed)
    key_hat = key_rows * growth
    key_tilde = key_rows * jnp.exp(-summed)
    query_estimate = query_rows * growth
    same_doc = doc_ids[:, None] == doc_ids[None, :]
    strict = same_doc & (row_index[:, None] > row_index[None, :])
    up_to = same_doc & (row_index[:, None] >= row_index[None, :])
    carried = (doc_ids == prev_doc).astype(jnp.float32)
    inner = jnp.einsum("hic,hjc->hij", key_hat, key_tilde, precision=top_value)
    lower_part = jnp.where(strict[None], inner * strength[:, :, None], 0.0)
    system = lower_part + jnp.eye(span_len, dtype=jnp.float32)[None]
    right_side = jnp.concatenate(
        [(strength * carried[None])[:, :, None] * key_hat, strength[:, :, None] * value_rows],
        axis=2,
    )
    solved = lax.linalg.triangular_solve(
        system, right_side, left_side=True, lower=True, unit_diagonal=True
    )
    weighted_key_rows = solved[:, :, :state_dim]
    update_rows = solved[:, :, state_dim:]
    attend = jnp.where(
        up_to[None], jnp.einsum("hic,hjc->hij", query_estimate, key_tilde, precision=top_value), 0.0
    )
    tail_mask = same_doc[span_len - 1].astype(jnp.float32)
    key_decay = key_rows * jnp.exp(summed[:, span_len - 1 :, :] - summed) * tail_mask[None, :, None]
    diagonal = (
        carried[span_len - 1]
        * growth[:, span_len - 1, :, None]
        * jnp.eye(state_dim, dtype=jnp.float32)[None]
    )
    transition = diagonal - jnp.einsum(
        "hjc,hjd->hcd", key_decay, weighted_key_rows, precision=top_value
    )
    offset = jnp.einsum("hjc,hjv->hcv", key_decay, update_rows, precision=top_value)
    return (query_estimate, carried, weighted_key_rows, update_rows, attend, transition, offset)


def span_output(terms, inbound_state):
    query_estimate, carried, weighted_key_rows, update_rows, attend, transition, offset = terms
    adjusted_rows = update_rows - jnp.einsum(
        "izy,iyn->izn", weighted_key_rows, inbound_state, precision=top_value
    )
    state_contribution = jnp.einsum(
        "izy,iyn->izn", query_estimate, inbound_state, precision=top_value
    )
    return carried[None, :, None] * state_contribution + jnp.einsum(
        "hij,hjv->hiv", attend, adjusted_rows, precision=top_value
    )


def apply_map(transition, offset, inbound_state):
    return jnp.einsum("hcd,hdv->hcv", transition, inbound_state, precision=top_value) + offset


def local(
    kda_query,
    kda_key,
    kda_value,
    log_decay,
    write_strength,
    mla_query,
    latents,
    value_up,
    out_proj,
    doc_lengths,
):
    tokens_dev = kda_query.shape[1]
    heads_dev = write_strength.shape[1]
    state_dim = kda_query.shape[2] // heads_dev
    ctx_count = lax.axis_size("ctx")
    ctx_place = lax.axis_index("ctx")
    first_pos = ctx_place * tokens_dev
    positions = first_pos + jnp.arange(tokens_dev, dtype=jnp.int32)
    doc_ends = jnp.cumsum(doc_lengths[0])
    doc_ids = doc_index(positions, doc_ends)

    def head_first(packed):
        return jnp.transpose(
            packed[0].astype(jnp.float32).reshape(tokens_dev, heads_dev, state_dim), (1, 0, 2)
        )

    query_rows = unit_length(head_first(kda_query))
    key_rows = unit_length(head_first(kda_key))
    value_rows = head_first(kda_value)
    decay_rows = head_first(log_decay)
    strength = write_strength[0]
    span_list = []
    eye_batch = jnp.broadcast_to(
        jnp.eye(state_dim, dtype=jnp.float32), (heads_dev, state_dim, state_dim)
    )
    transition = eye_batch
    offset = jnp.zeros((heads_dev, state_dim, state_dim), jnp.float32)
    for span_begin in range(0, tokens_dev, SPAN):
        span_stop = span_begin + SPAN
        prev_doc = doc_index(positions[span_begin : span_begin + 1] - 1, doc_ends)[0]
        terms = span_terms(
            query_rows[:, span_begin:span_stop],
            key_rows[:, span_begin:span_stop],
            value_rows[:, span_begin:span_stop],
            decay_rows[:, span_begin:span_stop],
            strength[:, span_begin:span_stop],
            doc_ids[span_begin:span_stop],
            prev_doc,
        )
        span_list.append(terms)
        offset = apply_map(terms[5], terms[6], offset)
        transition = jnp.einsum("hcd,hde->hce", terms[5], transition, precision=top_value)

    def relay(turn_index, inbound_state):
        outgoing = apply_map(transition, offset, inbound_state)
        return from_behind(outgoing.astype(jnp.bfloat16), "ctx", 1).astype(outgoing.dtype)

    inbound_state = lax.fori_loop(0, ctx_count - 1, relay, jnp.zeros_like(offset))
    pieces = []
    state_now = inbound_state
    for span_number, terms in enumerate(span_list):
        pieces.append(span_output(terms, state_now))
        if span_number + 1 < len(span_list):
            state_now = apply_map(terms[5], terms[6], state_now)
    kda_out = (
        jnp.transpose(jnp.concatenate(pieces, axis=1), (1, 0, 2))
        .reshape(1, tokens_dev, heads_dev * state_dim)
        .astype(jnp.bfloat16)
    )
    width = latents.shape[2]
    lat_dim = value_up.shape[1]
    score_scale = 1.0 / math.sqrt(NOPE + ROPE)
    query_flat = mla_query[0].reshape(tokens_dev * heads_dev, width)
    row_pos = jnp.repeat(positions, heads_dev)
    row_doc = jnp.repeat(doc_ids, heads_dev)
    row_total_count = tokens_dev * heads_dev
    row_peak = jnp.full((row_total_count,), masked_score, jnp.float32)
    block_rows = lax.all_gather(latents, "ctx", axis=1, tiled=True)[0]
    row_count = block_rows.shape[0]
    key_pos = jnp.arange(row_count, dtype=jnp.int32)
    key_doc = doc_index(key_pos, doc_ends)
    scores = (
        lax.dot_general(
            query_flat, block_rows, (((1,), (1,)), ((), ())), preferred_element_type=jnp.float32
        )
        * score_scale
    )
    allowed = (
        (key_pos[None, :] <= row_pos[:, None])
        & (key_pos[None, :] >= 0)
        & (key_doc[None, :] == row_doc[:, None])
    )
    new_peak = jnp.maximum(row_peak, jnp.max(jnp.where(allowed, scores, masked_score), axis=1))
    exponent = jnp.where(allowed, jnp.exp(scores - new_peak[:, None]), 0.0)
    row_total = jnp.sum(exponent, axis=1)
    weighted = jnp.dot(
        exponent.astype(jnp.bfloat16), block_rows[:, :lat_dim], preferred_element_type=jnp.float32
    )
    row_peak, row_total, weighted = (new_peak, row_total, weighted)
    context = (
        (weighted / row_total[:, None]).astype(jnp.bfloat16).reshape(tokens_dev, heads_dev, lat_dim)
    )
    head_out = jnp.einsum(
        "thl,hlv->thv", context, value_up, preferred_element_type=jnp.float32
    ).astype(jnp.bfloat16)
    head_out = head_out.reshape(tokens_dev, heads_dev * value_up.shape[2])
    mixed = lax.psum_scatter(
        jnp.dot(head_out, out_proj, preferred_element_type=jnp.float32).astype(jnp.bfloat16),
        "head",
        scatter_dimension=0,
        tiled=True,
    )
    return (kda_out, mixed[None])


def solution(mesh):
    placed = (
        P(("group", "req"), "ctx", "head"),
        P(("group", "req"), "ctx", "head"),
        P(("group", "req"), "ctx", "head"),
        P(("group", "req"), "ctx", "head"),
        P(("group", "req"), "head", "ctx"),
        P(("group", "req"), "ctx", "head"),
        P(("group", "req"), "ctx", None),
        P("head", None, None),
        P("head", None),
        P(("group", "req"), None),
    )
    return jax.shard_map(
        local,
        mesh=mesh,
        in_specs=placed,
        out_specs=(P(("group", "req"), "ctx", "head"), P(("group", "req"), ("ctx", "head"), None)),
        check_vma=False,
    )
```

profile of v0, /device:TPU:0, one launch (start us, length us, event | category | flops | bytes accessed | tf_op | source)
XLA Modules:
  0.0 443.5 jit_solution(2530594987979370844)
XLA Ops:
  7.2 1.0 reduce-window.4
  8.8 23.7 %all_gather.3 = bf16[1,768,576]{2,1,0:T(8,128)(2,1)S(1)} all-gather(bf16[1,192,576]{2,1,0:T(8,128)(2,1)} %param.20), channel_id=1, replica_groups=mesh['group'=2,'ctx'=4,'head'=2,'req'=2] {'ctx'}, dimensions={1}, use_global_device_ids=true | all-gather | bytes 1105920 | tf_op jit(solution)/shard_map/all_gather | solution.py:166
  32.5 7.0 %reshape_squeeze.3 = bf16[3072,576]{1,0:T(8,128)(2,1)} reshape(bf16[1,192,9216]{2,1,0:T(8,128)(2,1)} %param.19) | data formatting | bytes 7077888 | tf_op jit(solution)/shard_map/reshape;squeeze | solution.py:161
  39.4 6.7 %select_reduce_fusion = (f32[3072]{0:T(1024)S(1)}, f32[3072,768]{0,1:T(8,128)S(1)}) fusion(s32[3072]{0:T(1024)S(1)} %eq.140, s32[3072]{0:T(1024)S(1)} %le.114, s32[768]{0:T(1024)S(1)} %convert_reduce_fusion, bf16[3072,576]{1,0:T(8,128)(2,1)} %reshape_squeeze.3, bf16[1,768,576]{2,1,0:T(8,128)(2,1)S(1)} %all_gather.3), kind=kOutput, calls=%fused_computation.7 | convolution fusion | flops 2732061696 | bytes 13900800 | tf_op jit(solution)/shard_map/dot_general | solution.py:171
  46.2 3.6 fusion.6
  49.8 4.3 divide_convert_fusion
  54.2 3.7 fusion.20
  57.9 3.0 convolution_convert_fusion
  62.2 1.0 convolution_bitcast_fusion.2
  65.9 2.0 compare_convert_fusion.2
  69.7 1.3 convert_bitcast_fusion.1
  72.0 1.0 bitcast_multiply_fusion
  73.3 1.9 fusion.30
  75.2 80.0 %custom-call.8 = f32[16,1,64,64]{2,3,1,0:T(8,128)} custom-call(f32[16,1,64,64]{3,2,1,0:T(8,128)} %fusion.30), custom_call_target="InvertDiagBlocksLowerTriangular" | custom-call | tf_op jit(solution)/shard_map/triangular_solve/custom-call.1 | solution.py:49
  155.2 1.3 convert_bitcast_fusion
  157.8 2.8 broadcast_multiply_fusion.2
  160.6 1.4 slice_multiply_fusion.4
  162.0 1.1 fusion.52
  163.1 1.9 fusion.68
  165.1 1.3 slice_multiply_fusion.18
  166.3 2.1 convolution_subtract_fusion
  168.4 2.1 fusion.62
  170.5 2.0 convolution_add_fusion.5
  172.4 1.9 fusion.35
  174.3 80.2 %custom-call.7 = f32[16,1,64,64]{2,3,1,0:T(8,128)} custom-call(f32[16,1,64,64]{3,2,1,0:T(8,128)} %fusion.35), custom_call_target="InvertDiagBlocksLowerTriangular" | custom-call | tf_op jit(solution)/shard_map/triangular_solve/custom-call.1 | solution.py:49
  254.5 2.4 fusion.48
  256.9 2.9 fusion.66
  259.8 3.1 convolution_subtract_fusion.1
  262.9 1.9 fusion.40
  264.7 80.2 %custom-call.6 = f32[16,1,64,64]{2,3,1,0:T(8,128)} custom-call(f32[16,1,64,64]{3,2,1,0:T(8,128)} %fusion.40), custom_call_target="InvertDiagBlocksLowerTriangular" | custom-call | tf_op jit(solution)/shard_map/triangular_solve/custom-call.1 | solution.py:49
  344.9 1.4 slice_multiply_fusion.20
  346.4 3.1 convolution_add_fusion.4
  349.5 1.1 fusion.44
  350.6 2.1 convolution_subtract_fusion.2
  352.7 1.1 fusion.119
  353.9 3.0 convolution_add_fusion.3
  356.8 1.1 fusion.117
  358.0 2.2 fusion.118
  360.2 53.5 %while.11 = (s32[]{:T(128)}, f32[16,128,128]{2,1,0:T(8,128)S(1)}, f32[16,128,128]{2,1,0:T(8,128)}, f32[16,128,128]{2,1,0:T(8,128)}, s32[]{:T(128)}, /*index=5*/s32[]{:T(128)}) while((s32[]{:T(128)}, f32[16,128,128]{2,1,0:T(8,128)S(1)}, f32[16,128,128]{2,1,0:T(8,128)}, f32[16,128,128]{2,1,0:T(8,128)}, s32[]{:T(128)}, ...), condition=%wide.region_8.10_spmd.clone, body=%wide.region_7.9_spmd.clone.sunk | while | flops 403701760 | bytes 7340151 | solution.py:146
  360.2 3.5 fusion.158
  363.7 2.8 collective-permute-start
  366.5 9.6 %collective-permute-done = bf16[16,128,128]{2,1,0:T(8,128)(2,1)} collective-permute-done((bf16[16,128,128]{2,1,0:T(8,128)(2,1)}, bf16[16,128,128]{2,1,0:T(8,128)(2,1)}, u32[]{:S(2)}, u32[]{:S(2)}) %collective-permute-start) | collective-permute-done | bytes 524320 | tf_op jit(solution)/shard_map/while/body/eval_jaxpr/ppermute | solution.py:17
  376.1 1.1 convert_element_type.234
  377.3 3.5 fusion.158
  380.8 5.2 %collective-permute-start = (bf16[16,128,128]{2,1,0:T(8,128)(2,1)}, bf16[16,128,128]{2,1,0:T(8,128)(2,1)}, u32[]{:S(2)}, u32[]{:S(2)}) collective-permute-start(bf16[16,128,128]{2,1,0:T(8,128)(2,1)} %fusion.158), channel_id=1, source_target_pairs={{0,4},{4,8},{8,12},{1,5},{5,9},{9,13},{2,6},{6,10},{10,14},{3,7},{... | collective-permute-start | bytes 1572872 | tf_op jit(solution)/shard_map/while/body/eval_jaxpr/ppermute | solution.py:17
  385.9 8.7 %collective-permute-done = bf16[16,128,128]{2,1,0:T(8,128)(2,1)} collective-permute-done((bf16[16,128,128]{2,1,0:T(8,128)(2,1)}, bf16[16,128,128]{2,1,0:T(8,128)(2,1)}, u32[]{:S(2)}, u32[]{:S(2)}) %collective-permute-start) | collective-permute-done | bytes 524320 | tf_op jit(solution)/shard_map/while/body/eval_jaxpr/ppermute | solution.py:17
  394.7 1.1 convert_element_type.234
  395.8 3.5 fusion.158
  399.3 5.2 %collective-permute-start = (bf16[16,128,128]{2,1,0:T(8,128)(2,1)}, bf16[16,128,128]{2,1,0:T(8,128)(2,1)}, u32[]{:S(2)}, u32[]{:S(2)}) collective-permute-start(bf16[16,128,128]{2,1,0:T(8,128)(2,1)} %fusion.158), channel_id=1, source_target_pairs={{0,4},{4,8},{8,12},{1,5},{5,9},{9,13},{2,6},{6,10},{10,14},{3,7},{... | collective-permute-start | bytes 1572872 | tf_op jit(solution)/shard_map/while/body/eval_jaxpr/ppermute | solution.py:17
  404.5 7.8 %collective-permute-done = bf16[16,128,128]{2,1,0:T(8,128)(2,1)} collective-permute-done((bf16[16,128,128]{2,1,0:T(8,128)(2,1)}, bf16[16,128,128]{2,1,0:T(8,128)(2,1)}, u32[]{:S(2)}, u32[]{:S(2)}) %collective-permute-start) | collective-permute-done | bytes 524320 | tf_op jit(solution)/shard_map/while/body/eval_jaxpr/ppermute | solution.py:17
  412.3 1.1 convert_element_type.234
  413.7 2.4 convolution_subtract_fusion.5
  416.2 1.2 convolution_add_fusion.2
  417.4 1.1 convolution_subtract_fusion.4
  418.9 1.2 convolution_add_fusion.1
  422.3 1.0 convolution_select_fusion.2
  423.4 1.0 convolution_select_fusion.1
  424.6 1.1 convolution_subtract_fusion.3
  427.1 1.0 convolution_select_fusion
  429.1 1.1 fusion.43
  430.2 1.1 fusion.42
  431.4 1.1 fusion.41
  432.6 1.4 copy.39
  434.0 2.1 convert_element_type.184
  (112 shorter events, 12.2 us)
Async XLA Ops:
  7.2 47.0 %copy-start = (bf16[16,512,128]{2,1,0:T(8,128)(2,1)S(1)}, bf16[16,512,128]{2,1,0:T(8,128)(2,1)}, u32[]{:S(2)}) copy-start(bf16[16,512,128]{2,1,0:T(8,128)(2,1)} %param.21) | copy-start | bytes 6291460
  7.2 428.9 %reduce-scatter.2.cloned.1.call-start = ((), (), s32[]{:S(2)}) async-start(), calls=%async_computation.1 | async-start | bytes 1327104 | tf_op jit(solution)/shard_map/reduce_scatter | solution.py:195
  46.2 11.7 %slice-start = ((s8[9437184]{0:T(1024)(128)(4,1)}), s8[4194304]{0:T(1024)(128)(4,1)S(1)}, s32[]{:S(2)}) async-start(s8[9437184]{0:T(1024)(128)(4,1)} %bitcast.155), calls=%async_computation.2 | async-start | bytes 8388608
  49.8 8.1 %slice-start.1 = ((s8[9437184]{0:T(1024)(128)(4,1)}), s8[4194304]{0:T(1024)(128)(4,1)S(1)}, s32[]{:S(2)}) async-start(s8[9437184]{0:T(1024)(128)(4,1)} %bitcast.155), calls=%async_computation.3 | async-start | bytes 8388608
  49.8 8.1 %slice-start.2 = ((s8[9437184]{0:T(1024)(128)(4,1)}), s8[1048576]{0:T(1024)(128)(4,1)S(1)}, s32[]{:S(2)}) async-start(s8[9437184]{0:T(1024)(128)(4,1)} %bitcast.155), calls=%async_computation.4 | async-start | bytes 2097152
  57.9 3.6 copy-start.24
  61.7 7.9 %copy-start.28 = (f32[1,16,192]{2,1,0:T(8,128)S(1)}, f32[1,16,192]{2,1,0:T(8,128)}, u32[]{:S(2)}) copy-start(f32[1,16,192]{2,1,0:T(8,128)} %param.18) | copy-start | bytes 36868
  62.0 1.3 copy-start.21
  72.0 1.2 copy-start.2
  156.7 1.0 copy-start.3
  160.6 1.5 copy-start.26
  163.1 5.3 %copy-start.15 = (f32[16,64,256]{2,1,0:T(8,128)}, f32[16,64,256]{2,1,0:T(8,128)S(1)}, u32[]{:S(2)}) copy-start(f32[16,64,256]{2,1,0:T(8,128)S(1)} %fusion.52) | copy-start | bytes 3145732
  165.0 5.4 %copy-start.12 = (f32[16,128,128]{2,1,0:T(8,128)}, f32[16,128,128]{2,1,0:T(8,128)S(1)}, u32[]{:S(2)}) copy-start(f32[16,128,128]{2,1,0:T(8,128)S(1)} %fusion.68) | copy-start | bytes 3145732
  168.4 4.0 copy-start.8
  256.9 6.0 %copy-start.16 = (f32[16,64,256]{2,1,0:T(8,128)}, f32[16,64,256]{2,1,0:T(8,128)S(1)}, u32[]{:S(2)}) copy-start(f32[16,64,256]{2,1,0:T(8,128)S(1)} %fusion.48) | copy-start | bytes 3145732
  259.8 3.1 copy-start.5
  346.3 3.2 copy-start.22
  346.3 3.2 copy-start.23
  346.4 3.2 copy-start.27
  349.5 1.1 copy-start.6
  350.6 3.2 copy-start.18
  353.8 3.0 copy-start.10
  353.8 3.0 copy-start.20
  363.7 12.4 %collective-permute-start = (bf16[16,128,128]{2,1,0:T(8,128)(2,1)}, bf16[16,128,128]{2,1,0:T(8,128)(2,1)}, u32[]{:S(2)}, u32[]{:S(2)}) collective-permute-start(bf16[16,128,128]{2,1,0:T(8,128)(2,1)} %fusion.158), channel_id=1, source_target_pairs={{0,4},{4,8},{8,12},{1,5},{5,9},{9,13},{2,6},{6,10},{10,14},{3,7},{... | collective-permute-start | bytes 1572872 | tf_op jit(solution)/shard_map/while/body/eval_jaxpr/ppermute | solution.py:17
  380.8 13.9 %collective-permute-start = (bf16[16,128,128]{2,1,0:T(8,128)(2,1)}, bf16[16,128,128]{2,1,0:T(8,128)(2,1)}, u32[]{:S(2)}, u32[]{:S(2)}) collective-permute-start(bf16[16,128,128]{2,1,0:T(8,128)(2,1)} %fusion.158), channel_id=1, source_target_pairs={{0,4},{4,8},{8,12},{1,5},{5,9},{9,13},{2,6},{6,10},{10,14},{3,7},{... | collective-permute-start | bytes 1572872 | tf_op jit(solution)/shard_map/while/body/eval_jaxpr/ppermute | solution.py:17
  399.3 13.0 %collective-permute-start = (bf16[16,128,128]{2,1,0:T(8,128)(2,1)}, bf16[16,128,128]{2,1,0:T(8,128)(2,1)}, u32[]{:S(2)}, u32[]{:S(2)}) collective-permute-start(bf16[16,128,128]{2,1,0:T(8,128)(2,1)} %fusion.158), channel_id=1, source_target_pairs={{0,4},{4,8},{8,12},{1,5},{5,9},{9,13},{2,6},{6,10},{10,14},{3,7},{... | collective-permute-start | bytes 1572872 | tf_op jit(solution)/shard_map/while/body/eval_jaxpr/ppermute | solution.py:17
  413.7 2.4 copy-start.9
  413.7 2.4 copy-start.13
  416.2 1.2 copy-start.17
  417.4 1.2 copy-start.11
  417.4 1.5 copy-start.14
  418.9 1.2 copy-start.25
  421.3 1.0 copy-start.4
  423.4 1.2 copy-start.19
  425.7 1.3 copy-start.7
  432.5 3.6 copy-start.1
Sparse Core Ops, SparseCore 0:
  61.1 18.3 reduce-scatter.1
where the time goes:
time: 449 us; the launch traced here: 443 us
  other arithmetic  261 us (58%)
  matrix products  84.7 us (19%)
  waiting for transfers between devices  26.2 us (6%)
  blocking collectives  23.7 us (5%)
  between operations  17.1 us (4%)
  local copies, waits for them, and re-layouts  16.8 us (4%)
  starting transfers between devices  13.2 us (3%)
    another operation x5, other arithmetic, span_terms(): lax.linalg.triangular_solve(system, right_side, left_side=True, lower=Tru...  240 us
    ppermute x3, waiting for transfers between devices, from_behind(): return lax.ppermute(value, axis, pairs)  26.2 us
    all_gather x1, blocking collectives, local(): block_rows = lax.all_gather(latents, 'ctx', axis=1, tiled=True)[0]  23.7 us
    dot_general x8, matrix products, apply_map(): jnp.einsum('hcd,hdv->hcv', transition, inbound_state, precision=top_value)  19.1 us
    ppermute x3, starting transfers between devices, from_behind(): return lax.ppermute(value, axis, pairs)  13.1 us
  transfers between devices with their start and end apart: 4, of which 3 were waited for; matrix products, arithmetic and copies ran while one was open for 75% of the time, Pallas kernels for 0%

commit v1 on v0

--- a/solution.py
+++ b/solution.py
@@ -9,6 +9,30 @@
 SPAN = 64
 top_value = lax.Precision.HIGHEST
 masked_score = -1e30
+
+
+def get_the_edges(view, array_axis):
+    value_now = list(view.shape[1:])
+    value_now[array_axis] *= view.shape[0]
+    return jnp.moveaxis(view, 0, array_axis).reshape(value_now)
+
+
+def orders_link(m, group_axis):
+    fan = jax.lax.axis_size(group_axis)
+    top = m[None]
+    for no in range(fan.bit_length() - 1):
+        n_now = 1 << no
+        windows = []
+        dd = 0
+        while dd < fan:
+            windows.append((dd, dd ^ n_now))
+            dd += 1
+        v1 = jax.lax.ppermute(top, group_axis, windows)
+        p_next = jnp.stack([top, v1])
+        t_next = jax.lax.axis_index(group_axis)
+        back = t_next >> no & 1
+        top = jnp.where(back == 0, p_next, p_next[::-1]).reshape(-1, *m.shape)
+    return top
 
 
 def from_behind(value, axis, by):
@@ -163,7 +187,12 @@
     row_doc = jnp.repeat(doc_ids, heads_dev)
     row_total_count = tokens_dev * heads_dev
     row_peak = jnp.full((row_total_count,), masked_score, jnp.float32)
-    block_rows = lax.all_gather(latents, "ctx", axis=1, tiled=True)[0]
+
+    def convert_the_cubes(a0, k_dim, w_in):
+        fresh = orders_link(w_in, a0)
+        return get_the_edges(fresh, k_dim)
+
+    block_rows = convert_the_cubes("ctx", 1, latents)[0]
     row_count = block_rows.shape[0]
     key_pos = jnp.arange(row_count, dtype=jnp.int32)
     key_doc = doc_index(key_pos, doc_ends)

time: 449 us -> 469 us (1.045)
  blocking collectives: 23.7 us -> 0 us
  waiting for transfers between devices: 26.2 us -> 42 us
  other arithmetic: 261 us -> 271 us
  matrix products: 84.7 us -> 93.8 us
  starting transfers between devices: 13.2 us -> 20.8 us
    all_gather x1 -> x0, blocking collectives: 23.7 us -> none  [local(): block_rows = lax.all_gather(latents, 'ctx', axis=1, tiled=True)[0]]
    ppermute x0 -> x2, starting transfers between devices: none -> 7.36 us  [orders_link(): v1 = jax.lax.ppermute(top, group_axis, windows)]
    reduce_scatter x1, waiting for transfers between devices: 0.01 us -> 6.56 us  [local(): lax.psum_scatter(jnp.dot(head_out, out_proj, preferred_element_type=jnp.f...]
    ppermute x0 -> x2, waiting for transfers between devices: none -> 6.5 us  [orders_link(): v1 = jax.lax.ppermute(top, group_axis, windows)]
    dot_general x3, matrix products: 3.13 us -> 8.48 us  [span_terms(): jnp.einsum('hic,hjc->hij', query_estimate, key_tilde, precision=top_value)]
  transfers between devices with their start and end apart: 4 -> 6, of which waited for: 3 -> 5; matrix products, arithmetic and copies ran while one was open for 75% -> 78% of each run, Pallas kernels for 0% -> 0%
where the time goes in v1:
time: 469 us; the launch traced here: 464 us
  other arithmetic  271 us (58%)
  matrix products  93.8 us (20%)
  waiting for transfers between devices  42 us (9%)
  starting transfers between devices  20.8 us (4%)
  local copies, waits for them, and re-layouts  19.4 us (4%)
  between operations  17.5 us (4%)
    another operation x5, other arithmetic, span_terms(): lax.linalg.triangular_solve(system, right_side, left_side=True, lower=Tru...  242 us
    ppermute x3, waiting for transfers between devices, from_behind(): return lax.ppermute(value, axis, pairs)  28.9 us
    dot_general x8, matrix products, apply_map(): jnp.einsum('hcd,hdv->hcv', transition, inbound_state, precision=top_value)  20.1 us
    ppermute x3, starting transfers between devices, from_behind(): return lax.ppermute(value, axis, pairs)  13.4 us
  transfers between devices with their start and end apart: 6, of which 5 were waited for; matrix products, arithmetic and copies ran while one was open for 78% of the time, Pallas kernels for 0%

profile of v1, /device:TPU:0, one launch (start us, length us, event | category | flops | bytes accessed | tf_op | source)
XLA Modules:
  0.0 464.3 jit_solution(9635688585772101428)
XLA Ops:
  7.2 3.1 collective-permute-start.1
  10.3 1.3 copy.47
  18.2 1.9 compare_convert_fusion.2
  22.5 1.3 convert_bitcast_fusion.1
  27.6 1.9 fusion.33
  29.5 80.2 %custom-call.8 = f32[16,1,64,64]{2,3,1,0:T(8,128)} custom-call(f32[16,1,64,64]{3,2,1,0:T(8,128)} %fusion.33), custom_call_target="InvertDiagBlocksLowerTriangular" | custom-call | tf_op jit(solution)/shard_map/triangular_solve/custom-call.1 | solution.py:73
  109.7 1.3 convert_bitcast_fusion
  113.4 2.7 broadcast_multiply_fusion.2
  116.1 1.5 slice_multiply_fusion.4
  118.7 1.9 fusion.71
  120.6 1.2 slice_multiply_fusion.18
  121.9 2.1 convolution_subtract_fusion
  124.0 2.0 fusion.65
  125.9 2.0 convolution_add_fusion.5
  127.9 1.8 fusion.38
  129.8 80.2 %custom-call.7 = f32[16,1,64,64]{2,3,1,0:T(8,128)} custom-call(f32[16,1,64,64]{3,2,1,0:T(8,128)} %fusion.38), custom_call_target="InvertDiagBlocksLowerTriangular" | custom-call | tf_op jit(solution)/shard_map/triangular_solve/custom-call.1 | solution.py:73
  210.9 2.4 fusion.51
  213.3 2.9 fusion.69
  216.2 3.1 convolution_subtract_fusion.1
  219.3 1.8 fusion.43
  221.1 80.4 %custom-call.6 = f32[16,1,64,64]{2,3,1,0:T(8,128)} custom-call(f32[16,1,64,64]{3,2,1,0:T(8,128)} %fusion.43), custom_call_target="InvertDiagBlocksLowerTriangular" | custom-call | tf_op jit(solution)/shard_map/triangular_solve/custom-call.1 | solution.py:73
  302.3 1.4 slice_multiply_fusion.20
  303.7 3.1 convolution_add_fusion.4
  308.3 2.1 convolution_subtract_fusion.2
  310.4 1.1 fusion.122
  311.6 2.9 convolution_add_fusion.3
  314.5 1.1 fusion.120
  315.7 2.1 fusion.121
  317.8 56.5 %while.11 = (s32[]{:T(128)}, f32[16,128,128]{2,1,0:T(8,128)S(1)}, f32[16,128,128]{2,1,0:T(8,128)}, f32[16,128,128]{2,1,0:T(8,128)}, s32[]{:T(128)}, /*index=5*/s32[]{:T(128)}) while((s32[]{:T(128)}, f32[16,128,128]{2,1,0:T(8,128)S(1)}, f32[16,128,128]{2,1,0:T(8,128)}, f32[16,128,128]{2,1,0:T(8,128)}, s32[]{:T(128)}, ...), condition=%wide.region_8.10_spmd.clone, body=%wide.region_7.9_spmd.clone.sunk | while | flops 403701760 | bytes 7340151 | solution.py:170
  317.8 3.5 fusion.162
  321.3 2.8 collective-permute-start
  324.1 10.7 %collective-permute-done = bf16[16,128,128]{2,1,0:T(8,128)(2,1)} collective-permute-done((bf16[16,128,128]{2,1,0:T(8,128)(2,1)}, bf16[16,128,128]{2,1,0:T(8,128)(2,1)}, u32[]{:S(2)}, u32[]{:S(2)}) %collective-permute-start) | collective-permute-done | bytes 524320 | tf_op jit(solution)/shard_map/while/body/eval_jaxpr/ppermute | solution.py:41
  334.8 1.1 convert_element_type.234
  336.0 3.5 fusion.162
  339.5 5.4 %collective-permute-start = (bf16[16,128,128]{2,1,0:T(8,128)(2,1)}, bf16[16,128,128]{2,1,0:T(8,128)(2,1)}, u32[]{:S(2)}, u32[]{:S(2)}) collective-permute-start(bf16[16,128,128]{2,1,0:T(8,128)(2,1)} %fusion.162), channel_id=1, source_target_pairs={{0,4},{4,8},{8,12},{1,5},{5,9},{9,13},{2,6},{6,10},{10,14},{3,7},{... | collective-permute-start | bytes 1572872 | tf_op jit(solution)/shard_map/while/body/eval_jaxpr/ppermute | solution.py:41
  344.9 9.6 %collective-permute-done = bf16[16,128,128]{2,1,0:T(8,128)(2,1)} collective-permute-done((bf16[16,128,128]{2,1,0:T(8,128)(2,1)}, bf16[16,128,128]{2,1,0:T(8,128)(2,1)}, u32[]{:S(2)}, u32[]{:S(2)}) %collective-permute-start) | collective-permute-done | bytes 524320 | tf_op jit(solution)/shard_map/while/body/eval_jaxpr/ppermute | solution.py:41
  354.4 1.1 convert_element_type.234
  355.6 3.5 fusion.162
  359.1 5.2 %collective-permute-start = (bf16[16,128,128]{2,1,0:T(8,128)(2,1)}, bf16[16,128,128]{2,1,0:T(8,128)(2,1)}, u32[]{:S(2)}, u32[]{:S(2)}) collective-permute-start(bf16[16,128,128]{2,1,0:T(8,128)(2,1)} %fusion.162), channel_id=1, source_target_pairs={{0,4},{4,8},{8,12},{1,5},{5,9},{9,13},{2,6},{6,10},{10,14},{3,7},{... | collective-permute-start | bytes 1572872 | tf_op jit(solution)/shard_map/while/body/eval_jaxpr/ppermute | solution.py:41
  364.3 8.6 %collective-permute-done = bf16[16,128,128]{2,1,0:T(8,128)(2,1)} collective-permute-done((bf16[16,128,128]{2,1,0:T(8,128)(2,1)}, bf16[16,128,128]{2,1,0:T(8,128)(2,1)}, u32[]{:S(2)}, u32[]{:S(2)}) %collective-permute-start) | collective-permute-done | bytes 524320 | tf_op jit(solution)/shard_map/while/body/eval_jaxpr/ppermute | solution.py:41
  374.3 3.2 convolution_subtract_fusion.5
  377.5 1.2 convolution_add_fusion.2
  378.7 1.9 convolution_subtract_fusion.4
  380.6 2.1 convolution_add_fusion.1
  382.8 1.3 convert_bitcast_fusion.2
  385.1 1.7 bitcast_multiply_fusion.2
  386.8 2.7 convolution_select_fusion.2
  389.5 1.9 convolution_subtract_fusion.3
  392.6 4.3 collective-permute-start.2
  396.9 1.5 fusion.123
  398.7 7.1 %reshape_squeeze.3 = bf16[3072,576]{1,0:T(8,128)(2,1)} reshape(bf16[1,192,9216]{2,1,0:T(8,128)(2,1)} %param.19) | data formatting | bytes 7077888 | tf_op jit(solution)/shard_map/reshape;squeeze | solution.py:185
  406.0 3.4 convolution_select_fusion.1
  409.4 6.5 %collective-permute-done.2 = bf16[2,1,192,576]{3,2,0,1:T(8,128)(2,1)} collective-permute-done((bf16[2,1,192,576]{3,2,0,1:T(8,128)(2,1)}, bf16[2,1,192,576]{3,2,0,1:T(8,128)(2,1)}, u32[]{:S(2)}, u32[]{:S(2)}) %collective-permute-start.2) | collective-permute-done | bytes 442400 | tf_op jit(solution)/shard_map/ppermute | solution.py:30
  415.9 1.3 pad_maximum_fusion
  418.1 4.6 fusion.5
  422.8 3.7 fusion.9
  426.4 4.3 divide_convert_fusion
  430.8 3.7 fusion.23
  434.6 3.1 convolution_convert_fusion
  437.7 1.9 fusion.124
  439.6 2.4 convolution_select_fusion
  446.9 1.4 copy.39
  448.2 2.1 convert_element_type.184
  450.4 6.6 %reduce-scatter.2.cloned.1.call-done = bf16[96,2304]{1,0:T(8,128)(2,1)} async-done(((bf16[192,2304]{1,0:T(8,128)(2,1)}), bf16[96,2304]{1,0:T(8,128)(2,1)}) %reduce-scatter.2.cloned.1.call-update) | async-done | bytes 442384 | tf_op jit(solution)/shard_map/reduce_scatter | solution.py:224
  (197 shorter events, 26.8 us)
Async XLA Ops:
  7.2 423.6 %copy-start = (bf16[16,512,128]{2,1,0:T(8,128)(2,1)S(1)}, bf16[16,512,128]{2,1,0:T(8,128)(2,1)}, u32[]{:S(2)}) copy-start(bf16[16,512,128]{2,1,0:T(8,128)(2,1)} %param.21) | copy-start | bytes 6291460
  7.2 449.8 %reduce-scatter.2.cloned.1.call-start = ((), (), s32[]{:S(2)}) async-start(), calls=%async_computation.1 | async-start | bytes 1327104 | tf_op jit(solution)/shard_map/reduce_scatter | solution.py:224
  7.2 384.2 %collective-permute-start.1 = (bf16[1,1,192,576]{3,2,1,0:T(8,128)(2,1)}, bf16[1,1,192,576]{3,2,1,0:T(8,128)(2,1)S(1)}, u32[]{:S(2)}, u32[]{:S(2)}) collective-permute-start(bf16[1,1,192,576]{3,2,1,0:T(8,128)(2,1)} %bitcast.165), channel_id=1, source_target_pairs={{0,4},{4,0},{8,12},{12,8},{1,5},{5,1},{9,13},{13,9},{2,6},{6,2},{1... | collective-permute-start | bytes 663560 | tf_op jit(solution)/shard_map/ppermute | solution.py:30
  11.6 5.5 %copy-start.67 = (s32[1,8]{1,0:T(1,128)S(1)}, s32[1,8]{1,0:T(1,128)}, u32[]{:S(2)}) copy-start(s32[1,8]{1,0:T(1,128)} %param.23) | copy-start | bytes 100
  11.6 10.2 %copy-start.45 = (f32[1,16,192]{2,1,0:T(8,128)S(1)}, f32[1,16,192]{2,1,0:T(8,128)}, u32[]{:S(2)}) copy-start(f32[1,16,192]{2,1,0:T(8,128)} %param.18) | copy-start | bytes 36868
  11.8 2.7 copy-start.33
  14.6 9.5 %copy-start.56 = (s32[192]{0:T(256)}, s32[192]{0:T(256)S(1)}, u32[]{:S(2)}) copy-start(s32[192]{0:T(256)S(1)} %iota_add_fusion) | copy-start | bytes 2308
  17.4 6.7 %copy-start.54 = (s32[192]{0:T(256)}, s32[192]{0:T(256)S(1)}, u32[]{:S(2)}) copy-start(s32[192]{0:T(256)S(1)} %convert_reduce_fusion.1) | copy-start | bytes 2308
  20.1 4.0 copy-start.58
  20.1 4.0 copy-start.60
  20.1 4.0 copy-start.62
  25.4 2.2 copy-start.1
  111.3 1.5 copy-start.5
  111.3 2.1 copy-start.2
  111.3 2.1 copy-start.9
  111.3 2.1 copy-start.50
  111.3 2.1 copy-start.51
  111.3 2.1 copy-start.52
  118.7 5.2 %copy-start.26 = (f32[16,64,256]{2,1,0:T(8,128)}, f32[16,64,256]{2,1,0:T(8,128)S(1)}, u32[]{:S(2)}) copy-start(f32[16,64,256]{2,1,0:T(8,128)S(1)} %fusion.55) | copy-start | bytes 3145732
  120.6 5.3 %copy-start.23 = (f32[16,128,128]{2,1,0:T(8,128)}, f32[16,128,128]{2,1,0:T(8,128)S(1)}, u32[]{:S(2)}) copy-start(f32[16,128,128]{2,1,0:T(8,128)S(1)} %fusion.71) | copy-start | bytes 3145732
  124.0 4.0 copy-start.14
  125.9 2.0 copy-start.53
  129.8 83.5 %copy-start.44 = (f32[16,1,128]{2,1,0:T(1,128)S(1)}, f32[16,1,128]{2,1,0:T(1,128)}, u32[]{:S(2)}) copy-start(f32[16,1,128]{2,1,0:T(1,128)} %slice.175) | copy-start | bytes 24580
  210.0 3.3 copy-start.3
  210.0 3.3 copy-start.6
  213.3 6.0 %copy-start.27 = (f32[16,64,256]{2,1,0:T(8,128)}, f32[16,64,256]{2,1,0:T(8,128)S(1)}, u32[]{:S(2)}) copy-start(f32[16,64,256]{2,1,0:T(8,128)S(1)} %fusion.51) | copy-start | bytes 3145732
  216.2 3.1 copy-start.11
  216.2 3.1 copy-start.49
  303.7 3.2 copy-start.36
  303.7 3.2 copy-start.38
  303.7 3.2 copy-start.41
  307.9 3.6 copy-start.29
  311.6 2.9 copy-start.18
  311.6 2.9 copy-start.31
  321.3 13.5 %collective-permute-start = (bf16[16,128,128]{2,1,0:T(8,128)(2,1)}, bf16[16,128,128]{2,1,0:T(8,128)(2,1)}, u32[]{:S(2)}, u32[]{:S(2)}) collective-permute-start(bf16[16,128,128]{2,1,0:T(8,128)(2,1)} %fusion.162), channel_id=1, source_target_pairs={{0,4},{4,8},{8,12},{1,5},{5,9},{9,13},{2,6},{6,10},{10,14},{3,7},{... | collective-permute-start | bytes 1572872 | tf_op jit(solution)/shard_map/while/body/eval_jaxpr/ppermute | solution.py:41
  339.5 15.0 %collective-permute-start = (bf16[16,128,128]{2,1,0:T(8,128)(2,1)}, bf16[16,128,128]{2,1,0:T(8,128)(2,1)}, u32[]{:S(2)}, u32[]{:S(2)}) collective-permute-start(bf16[16,128,128]{2,1,0:T(8,128)(2,1)} %fusion.162), channel_id=1, source_target_pairs={{0,4},{4,8},{8,12},{1,5},{5,9},{9,13},{2,6},{6,10},{10,14},{3,7},{... | collective-permute-start | bytes 1572872 | tf_op jit(solution)/shard_map/while/body/eval_jaxpr/ppermute | solution.py:41
  359.1 13.8 %collective-permute-start = (bf16[16,128,128]{2,1,0:T(8,128)(2,1)}, bf16[16,128,128]{2,1,0:T(8,128)(2,1)}, u32[]{:S(2)}, u32[]{:S(2)}) collective-permute-start(bf16[16,128,128]{2,1,0:T(8,128)(2,1)} %fusion.162), channel_id=1, source_target_pairs={{0,4},{4,8},{8,12},{1,5},{5,9},{9,13},{2,6},{6,10},{10,14},{3,7},{... | collective-permute-start | bytes 1572872 | tf_op jit(solution)/shard_map/while/body/eval_jaxpr/ppermute | solution.py:41
  374.2 3.2 copy-start.15
  374.3 3.2 copy-start.24
  378.7 1.9 copy-start.16
  378.7 1.9 copy-start.19
  378.7 1.9 copy-start.25
  385.1 1.7 copy-start.48
  386.8 2.7 copy-start.21
  386.8 2.7 copy-start.30
  389.5 1.9 copy-start.42
  391.4 5.5 %copy-start.37 = (f32[16,64,128]{2,1,0:T(8,128)S(1)}, f32[16,64,128]{2,1,0:T(8,128)}, u32[]{:S(2)}) copy-start(f32[16,64,128]{2,1,0:T(8,128)} %convolution_subtract_fusion.5) | copy-start | bytes 1572868
  391.5 6.8 %copy-start.55 = (s32[192]{0:T(256)S(1)}, s32[192]{0:T(256)}, u32[]{:S(2)}) copy-start(s32[192]{0:T(256)} %copy-done.54) | copy-start | bytes 2308
  391.5 7.0 %copy-start.57 = (s32[192]{0:T(256)S(1)}, s32[192]{0:T(256)}, u32[]{:S(2)}) copy-start(s32[192]{0:T(256)} %copy-done.56) | copy-start | bytes 2308
  392.6 23.3 %collective-permute-start.2 = (bf16[2,1,192,576]{3,2,0,1:T(8,128)(2,1)}, bf16[2,1,192,576]{3,2,0,1:T(8,128)(2,1)}, u32[]{:S(2)}, u32[]{:S(2)}) collective-permute-start(bf16[2,1,192,576]{3,2,0,1:T(8,128)(2,1)} %get-tuple-element.62), channel_id=1, source_target_pairs={{0,8},{4,12},{8,0},{12,4},{1,9},{5,13},{9,1},{13,5},{2,10},{6,14},... | collective-permute-start | bytes 1327112 | tf_op jit(solution)/shard_map/ppermute | solution.py:30
  398.7 7.2 %copy-start.65 = (s32[8,1]{0,1:T(1,128)S(1)}, s32[8,1]{0,1:T(1,128)}, u32[]{:S(2)}) copy-start(s32[8,1]{0,1:T(1,128)} %copy-done.64) | copy-start | bytes 100
  398.7 7.2 %copy-start.47 = (pred[64,64]{1,0:T(8,128)(4,1)S(1)}, pred[64,64]{1,0:T(8,128)(4,1)}, u32[]{:S(2)}) copy-start(pred[64,64]{1,0:T(8,128)(4,1)} %get-tuple-element.92) | copy-start | bytes 12292
  405.9 10.0 %copy-start.39 = (bf16[1,2,1,192,576]{4,3,1,2,0:T(8,128)(2,1)S(1)}, bf16[1,2,1,192,576]{4,3,1,2,0:T(8,128)(2,1)}, u32[]{:S(2)}) copy-start(bf16[1,2,1,192,576]{4,3,1,2,0:T(8,128)(2,1)} %get-tuple-element.61) | copy-start | bytes 1327108
  415.9 2.3 copy-start.32
  422.7 11.8 %slice-start = ((s8[9437184]{0:T(1024)(128)(4,1)}), s8[4194304]{0:T(1024)(128)(4,1)S(1)}, s32[]{:S(2)}) async-start(s8[9437184]{0:T(1024)(128)(4,1)} %bitcast.180), calls=%async_computation.2 | async-start | bytes 8388608
  426.4 8.1 %slice-start.1 = ((s8[9437184]{0:T(1024)(128)(4,1)}), s8[4194304]{0:T(1024)(128)(4,1)S(1)}, s32[]{:S(2)}) async-start(s8[9437184]{0:T(1024)(128)(4,1)} %bitcast.180), calls=%async_computation.3 | async-start | bytes 8388608
  426.4 8.1 %slice-start.2 = ((s8[9437184]{0:T(1024)(128)(4,1)}), s8[1048576]{0:T(1024)(128)(4,1)S(1)}, s32[]{:S(2)}) async-start(s8[9437184]{0:T(1024)(128)(4,1)} %bitcast.180), calls=%async_computation.4 | async-start | bytes 2097152
  437.6 1.9 copy-start.46
  437.7 1.9 copy-start.13
  439.6 2.5 copy-start.34
  439.6 3.4 copy-start.10
  439.6 3.4 copy-start.20
  439.6 3.4 copy-start.35
  439.6 3.4 copy-start.63
  (13 other events, 16.9 us)
Sparse Core Ops, SparseCore 0:
  437.8 19.1 reduce-scatter.1
